TPU v7x, 32 devices: a whole 2x2x4 slice. The times are simulated.
32 devices in a mesh: section: 4 (over x, core), row: 4 (over z), col: 2 (over y).
Axes of the slice: x: 2, y: 2, z: 4, core: 2. Of those that a mesh axis runs over, the one named last changes fastest.
Arguments:
- latents: bfloat16 [2, 1280, 4, 128], P(None, 'col', 'row'), may hold values from -6 to 6
- timesteps: int32 [2], replicated, may hold values from 0 to 999
- weights: bfloat16 [4, 1280, 1280], P('section', 'row', 'col'), may hold values from -0.15625 to 0.15625
- taps: float32 [4, 3, 1280], P('section'), may hold values from -3 to 3
- time_table: bfloat16 [4, 1000, 1280], P('section'), may hold values from -5 to 5
- dilations: int32 [4], P('section'), may hold values from 1 to 4
Outputs:
- acts: bfloat16 [4, 2, 1280, 4, 128], P('section', None, 'col', 'row')
All inputs are finite; a program needn't handle non-finite values.
Results may differ from a plain program's by a relative error of at most 0.03.
Values may be sent and summed in bfloat16 or wider, within the bound.
A program may use at most 64 MiB of HBM per device.

v0:
```python
import jax
import jax.numpy as jnp
from jax import lax
from jax.sharding import PartitionSpec as P

DMAX = 4


def shifted(value, axis, steps):
    count = lax.axis_size(axis)
    first, last = (max(0, -steps), min(count, count - steps))
    return lax.ppermute(value, axis, [(source, source + steps) for source in range(first, last)])


def from_partner(block, axis, distance):
    count = lax.axis_size(axis)
    route = []
    for low in range(count):
        high = low | 1 << distance
        if high != low and high < count:
            route += [(low, high), (high, low)]
    return lax.ppermute(block, axis, route)


def activate(current, tap_rows, embedding, dilation, frame_count):
    widened = current.astype(jnp.float32)
    padded = jnp.pad(widened, ((0, 0), (0, 0), (DMAX, DMAX)))
    earlier = lax.dynamic_slice_in_dim(padded, DMAX - dilation, frame_count, 2)
    later_frames = lax.dynamic_slice_in_dim(padded, DMAX + dilation, frame_count, 2)
    summed = (
        tap_rows[0][:, None, None] * earlier
        + tap_rows[1][:, None, None] * widened
        + tap_rows[2][:, None, None] * later_frames
        + embedding[:, None, None]
    )
    return jax.nn.silu(summed).astype(jnp.bfloat16)


def per_device(latents, timesteps, weights, taps, time_table, dilations):
    section_count = lax.axis_size("section")
    section_id = lax.axis_index("section")
    col_index = lax.axis_index("col")
    micro_count = latents.shape[0]
    local_channels = latents.shape[1]
    frame_count = latents.shape[3]
    midpoint = section_count // 2
    bit_total = section_count.bit_length() - 1
    matrix_cols = lax.all_gather(weights[0], "row", axis=0, tiled=True)
    tap_all = taps[0]
    time_rows = time_table[0]
    dilation = dilations[0]

    def advance(tick_id, state_tuple, with_skip):
        incoming, kept, skip_store = state_tuple
        micro_id = tick_id - section_id
        active = (micro_id >= 0) & (micro_id < micro_count)
        slot_id = jnp.clip(micro_id, 0, micro_count - 1)
        entering = lax.dynamic_index_in_dim(latents, slot_id, 0, keepdims=False)
        current = jnp.where(section_id == 0, entering, incoming)
        step_id = lax.dynamic_index_in_dim(timesteps, slot_id, 0, keepdims=False)
        embedding = lax.dynamic_index_in_dim(time_rows, step_id, 0, keepdims=False).astype(
            jnp.float32
        )
        tap_mine = lax.dynamic_slice_in_dim(tap_all, col_index * local_channels, local_channels, 1)
        embed_mine = lax.dynamic_slice_in_dim(
            embedding, col_index * local_channels, local_channels, 0
        )
        activated = lax.all_gather(
            activate(current, tap_mine, embed_mine, dilation, frame_count),
            "col",
            axis=0,
            tiled=True,
        )
        mixed = lax.dot_general(
            matrix_cols,
            activated.reshape(activated.shape[0], -1),
            (((0,), (0,)), ((), ())),
            preferred_element_type=jnp.float32,
        ).reshape(current.shape)
        stored_skip = lax.dynamic_index_in_dim(skip_store, slot_id, 0, keepdims=False).astype(
            jnp.float32
        )
        skip_term = jnp.where(section_id >= midpoint, stored_skip, 0.0)
        result = (current.astype(jnp.float32) + mixed + skip_term).astype(jnp.bfloat16)
        previous = lax.dynamic_index_in_dim(kept, slot_id, 0, keepdims=False)
        kept = lax.dynamic_update_index_in_dim(
            kept, jnp.where(active, result, previous), slot_id, 0
        )
        incoming = shifted(result, "section", 1)
        if with_skip:
            mirrored = result
            bit_order = list(range(bit_total))
            for bit_number in bit_order:
                mirrored = from_partner(mirrored, "section", bit_number)
            source_micro = tick_id - (section_count - 1 - section_id)
            usable = (section_id >= midpoint) & (source_micro >= 0) & (source_micro < micro_count)
            source_slot = jnp.clip(source_micro, 0, micro_count - 1)
            held = lax.dynamic_index_in_dim(skip_store, source_slot, 0, keepdims=False)
            skip_store = lax.dynamic_update_index_in_dim(
                skip_store, jnp.where(usable, mirrored, held), source_slot, 0
            )
        return (incoming, kept, skip_store)

    blank = jnp.zeros(latents.shape[1:], jnp.bfloat16)
    initial = (
        blank,
        jnp.zeros(latents.shape, jnp.bfloat16),
        jnp.zeros(latents.shape, jnp.bfloat16),
    )
    first_end = micro_count + midpoint - 1
    state_tuple = lax.fori_loop(
        0, first_end, lambda tick_id, carried: advance(tick_id, carried, True), initial
    )
    state_tuple = lax.fori_loop(
        first_end,
        micro_count + section_count - 1,
        lambda tick_id, carried: advance(tick_id, carried, False),
        state_tuple,
    )
    return state_tuple[1][None]


def solution(mesh):
    in_specs = (
        P(None, "col", "row", None),
        P(),
        P("section", "row", "col"),
        P("section", None, None),
        P("section", None, None),
        P("section"),
    )
    out_specs = P("section", None, "col", "row", None)
    return jax.shard_map(
        per_device, mesh=mesh, in_specs=in_specs, out_specs=out_specs, check_vma=False
    )
```

profile of v0, /device:TPU:1, one launch (start us, length us, event | category | flops | bytes accessed | tf_op | source)
XLA Modules:
  0.0 153.2 jit_solution(2454798220183565018)
XLA Ops:
  6.5 0.7 all-gather.3.cloned.1.call-update
  8.0 1.2 copy.7
  9.2 40.0 %all-gather.3.cloned.1.call-done = bf16[1,1280,640]{2,1,0:T(8,128)(2,1)} async-done(((bf16[1,320,640]{2,1,0:T(8,128)(2,1)}), bf16[1,1280,640]{2,1,0:T(8,128)(2,1)}) %all-gather.3.cloned.1.call-update) | async-done | bytes 1638416 | tf_op jit(solution)/shard_map/all_gather | solution.py:48
  49.2 61.1 %while.38 = (s32[]{:T(128)}, bf16[640,1,128]{0,2,1:T(8,128)(2,1)S(1)}, bf16[2,640,1,128]{1,3,2,0:T(8,128)(2,1)S(1)}, bf16[2,640,1,128]{1,3,2,0:T(8,128)(2,1)S(1)...) while((s32[]{:T(128)}, ...), condition=%wide.region_1.2_spmd, body=%wide.region_0.1_spmd.sunk | while | flops 211354256 | bytes 14284052 | solution.py:111
  49.3 0.6 dynamic_slice.274
  51.9 0.8 slice_reduce_fusion.8
  52.9 5.7 %all_gather.28 = bf16[1280,1,128]{0,2,1:T(8,128)(2,1)S(1)} all-gather(bf16[640,1,128]{0,2,1:T(8,128)(2,1)S(1)} %multiply_convert_fusion.4), channel_id=1, replica_groups=mesh['section'=4,'row'=4,'col'=2] {'col'}, dimensions={0}, use_global_device_ids=true | all-gather | bytes 491520 | tf_op jit(solution)/shard_map/while/body/eval_jaxpr/all_gather | solution.py:68
  58.6 1.1 bitcast_dynamic-update-slice_fusion.6
  59.7 1.6 %collective-permute-start.1 = (bf16[640,1,128]{0,2,1:T(8,128)(2,1)}, bf16[640,1,128]{0,2,1:T(8,128)(2,1)S(1)}, u32[]{:S(2)}, u32[]{:S(2)}) collective-permute-start(bf16[640,1,128]{0,2,1:T(8,128)(2,1)} %get-tuple-element.1072), channel_id=1, source_target_pairs={{0,8},{8,0},{16,24},{24,16},{1,9},{9,1},{17,25},{25,17},{2,10},{10... | collective-permute-start | bytes 491528 | tf_op jit(solution)/shard_map/while/body/eval_jaxpr/ppermute | solution.py:22
  61.3 1.2 collective-permute-done.1
  62.5 1.2 collective-permute-start.2
  63.7 2.7 %collective-permute-start = (bf16[640,1,128]{0,2,1:T(8,128)(2,1)}, bf16[640,1,128]{0,2,1:T(8,128)(2,1)S(1)}, u32[]{:S(2)}, u32[]{:S(2)}) collective-permute-start(bf16[640,1,128]{0,2,1:T(8,128)(2,1)} %get-tuple-element.1072), channel_id=1, source_target_pairs={{0,8},{8,16},{16,24},{1,9},{9,17},{17,25},{2,10},{10,18},{18,26},{... | collective-permute-start | bytes 491528 | tf_op jit(solution)/shard_map/while/body/eval_jaxpr/ppermute | solution.py:12
  66.5 1.5 collective-permute-done.2
  68.0 1.6 %collective-permute-done = bf16[640,1,128]{0,2,1:T(8,128)(2,1)S(1)} collective-permute-done((bf16[640,1,128]{0,2,1:T(8,128)(2,1)}, bf16[640,1,128]{0,2,1:T(8,128)(2,1)S(1)}, u32[]{:S(2)}, u32[]{:S(2)}) %collective-permute-start) | collective-permute-done | bytes 163872 | tf_op jit(solution)/shard_map/while/body/eval_jaxpr/ppermute | solution.py:12
  69.6 0.6 dynamic_slice.274
  72.2 0.8 slice_reduce_fusion.8
  73.2 6.8 %all_gather.28 = bf16[1280,1,128]{0,2,1:T(8,128)(2,1)S(1)} all-gather(bf16[640,1,128]{0,2,1:T(8,128)(2,1)S(1)} %multiply_convert_fusion.4), channel_id=1, replica_groups=mesh['section'=4,'row'=4,'col'=2] {'col'}, dimensions={0}, use_global_device_ids=true | all-gather | bytes 491520 | tf_op jit(solution)/shard_map/while/body/eval_jaxpr/all_gather | solution.py:68
  80.0 1.1 bitcast_dynamic-update-slice_fusion.6
  81.1 0.5 collective-permute-start.1
  81.6 1.2 collective-permute-done.1
  82.9 1.2 collective-permute-start.2
  84.1 2.7 %collective-permute-start = (bf16[640,1,128]{0,2,1:T(8,128)(2,1)}, bf16[640,1,128]{0,2,1:T(8,128)(2,1)S(1)}, u32[]{:S(2)}, u32[]{:S(2)}) collective-permute-start(bf16[640,1,128]{0,2,1:T(8,128)(2,1)} %get-tuple-element.1072), channel_id=1, source_target_pairs={{0,8},{8,16},{16,24},{1,9},{9,17},{17,25},{2,10},{10,18},{18,26},{... | collective-permute-start | bytes 491528 | tf_op jit(solution)/shard_map/while/body/eval_jaxpr/ppermute | solution.py:12
  86.8 1.5 collective-permute-done.2
  88.4 1.6 %collective-permute-done = bf16[640,1,128]{0,2,1:T(8,128)(2,1)S(1)} collective-permute-done((bf16[640,1,128]{0,2,1:T(8,128)(2,1)}, bf16[640,1,128]{0,2,1:T(8,128)(2,1)S(1)}, u32[]{:S(2)}, u32[]{:S(2)}) %collective-permute-start) | collective-permute-done | bytes 163872 | tf_op jit(solution)/shard_map/while/body/eval_jaxpr/ppermute | solution.py:12
  90.0 0.6 dynamic_slice.274
  92.5 0.8 slice_reduce_fusion.8
  93.6 6.8 %all_gather.28 = bf16[1280,1,128]{0,2,1:T(8,128)(2,1)S(1)} all-gather(bf16[640,1,128]{0,2,1:T(8,128)(2,1)S(1)} %multiply_convert_fusion.4), channel_id=1, replica_groups=mesh['section'=4,'row'=4,'col'=2] {'col'}, dimensions={0}, use_global_device_ids=true | all-gather | bytes 491520 | tf_op jit(solution)/shard_map/while/body/eval_jaxpr/all_gather | solution.py:68
  100.4 1.1 bitcast_dynamic-update-slice_fusion.6
  101.5 0.5 collective-permute-start.1
  102.0 1.2 collective-permute-done.1
  103.2 1.2 collective-permute-start.2
  104.4 2.7 %collective-permute-start = (bf16[640,1,128]{0,2,1:T(8,128)(2,1)}, bf16[640,1,128]{0,2,1:T(8,128)(2,1)S(1)}, u32[]{:S(2)}, u32[]{:S(2)}) collective-permute-start(bf16[640,1,128]{0,2,1:T(8,128)(2,1)} %get-tuple-element.1072), channel_id=1, source_target_pairs={{0,8},{8,16},{16,24},{1,9},{9,17},{17,25},{2,10},{10,18},{18,26},{... | collective-permute-start | bytes 491528 | tf_op jit(solution)/shard_map/while/body/eval_jaxpr/ppermute | solution.py:12
  107.2 1.5 collective-permute-done.2
  108.7 1.6 %collective-permute-done = bf16[640,1,128]{0,2,1:T(8,128)(2,1)S(1)} collective-permute-done((bf16[640,1,128]{0,2,1:T(8,128)(2,1)}, bf16[640,1,128]{0,2,1:T(8,128)(2,1)S(1)}, u32[]{:S(2)}, u32[]{:S(2)}) %collective-permute-start) | collective-permute-done | bytes 163872 | tf_op jit(solution)/shard_map/while/body/eval_jaxpr/ppermute | solution.py:12
  110.3 35.1 %while.39 = (s32[]{:T(128)}, bf16[640,1,128]{0,2,1:T(8,128)(2,1)S(1)}, bf16[2,640,1,128]{1,3,2,0:T(8,128)(2,1)S(1)}, pred[]{:T(512)}, s32[]{:T(128)}, /*index=5*...) while((s32[]{:T(128)}, ...), condition=%wide.region_3.4_spmd, body=%wide.region_2.3_spmd.sunk | while | flops 211272336 | bytes 12153995 | solution.py:114
  110.3 0.6 dynamic_slice.279
  112.9 0.8 slice_reduce_fusion.9
  113.9 6.8 %all_gather.29 = bf16[1280,1,128]{0,2,1:T(8,128)(2,1)S(1)} all-gather(bf16[640,1,128]{0,2,1:T(8,128)(2,1)S(1)} %multiply_convert_fusion.5), channel_id=1, replica_groups=mesh['section'=4,'row'=4,'col'=2] {'col'}, dimensions={0}, use_global_device_ids=true | all-gather | bytes 491520 | tf_op jit(solution)/shard_map/while/body/eval_jaxpr/all_gather | solution.py:68
  120.7 1.1 bitcast_dynamic-update-slice_fusion.8
  121.8 3.5 %collective-permute-start.3 = (bf16[640,1,128]{0,2,1:T(8,128)(2,1)}, bf16[640,1,128]{0,2,1:T(8,128)(2,1)S(1)}, u32[]{:S(2)}, u32[]{:S(2)}) collective-permute-start(bf16[640,1,128]{0,2,1:T(8,128)(2,1)} %get-tuple-element.1093), channel_id=1, source_target_pairs={{0,8},{8,16},{16,24},{1,9},{9,17},{17,25},{2,10},{10,18},{18,26},{... | collective-permute-start | bytes 491528 | tf_op jit(solution)/shard_map/while/body/eval_jaxpr/ppermute | solution.py:12
  125.3 2.6 %collective-permute-done.3 = bf16[640,1,128]{0,2,1:T(8,128)(2,1)S(1)} collective-permute-done((bf16[640,1,128]{0,2,1:T(8,128)(2,1)}, bf16[640,1,128]{0,2,1:T(8,128)(2,1)S(1)}, u32[]{:S(2)}, u32[]{:S(2)}) %collective-permute-start.3) | collective-permute-done | bytes 163872 | tf_op jit(solution)/shard_map/while/body/eval_jaxpr/ppermute | solution.py:12
  127.9 0.6 dynamic_slice.279
  130.5 0.8 slice_reduce_fusion.9
  131.5 4.8 %all_gather.29 = bf16[1280,1,128]{0,2,1:T(8,128)(2,1)S(1)} all-gather(bf16[640,1,128]{0,2,1:T(8,128)(2,1)S(1)} %multiply_convert_fusion.5), channel_id=1, replica_groups=mesh['section'=4,'row'=4,'col'=2] {'col'}, dimensions={0}, use_global_device_ids=true | all-gather | bytes 491520 | tf_op jit(solution)/shard_map/while/body/eval_jaxpr/all_gather | solution.py:68
  136.4 1.1 bitcast_dynamic-update-slice_fusion.8
  137.5 5.4 %collective-permute-start.3 = (bf16[640,1,128]{0,2,1:T(8,128)(2,1)}, bf16[640,1,128]{0,2,1:T(8,128)(2,1)S(1)}, u32[]{:S(2)}, u32[]{:S(2)}) collective-permute-start(bf16[640,1,128]{0,2,1:T(8,128)(2,1)} %get-tuple-element.1093), channel_id=1, source_target_pairs={{0,8},{8,16},{16,24},{1,9},{9,17},{17,25},{2,10},{10,18},{18,26},{... | collective-permute-start | bytes 491528 | tf_op jit(solution)/shard_map/while/body/eval_jaxpr/ppermute | solution.py:12
  142.9 2.6 %collective-permute-done.3 = bf16[640,1,128]{0,2,1:T(8,128)(2,1)S(1)} collective-permute-done((bf16[640,1,128]{0,2,1:T(8,128)(2,1)}, bf16[640,1,128]{0,2,1:T(8,128)(2,1)S(1)}, u32[]{:S(2)}, u32[]{:S(2)}) %collective-permute-start.3) | collective-permute-done | bytes 163872 | tf_op jit(solution)/shard_map/while/body/eval_jaxpr/ppermute | solution.py:12
  145.5 0.9 copy.9
  (41 shorter events, 1.6 us)
Async XLA Ops:
  6.5 1.4 copy-start
  6.5 42.7 %copy-start.3 = (s32[2]{0:T(128)S(1)}, s32[2]{0:T(128)}, u32[]{:S(2)}) copy-start(s32[2]{0:T(128)} %param.11) | copy-start | bytes 28
  6.5 42.6 %all-gather.3.cloned.1.call-start = ((), (), s32[]{:S(2)}) async-start(), calls=%async_computation | async-start | bytes 2048000 | tf_op jit(solution)/shard_map/all_gather | solution.py:48
  49.3 9.3 %copy-start.1 = (bf16[1280,640]{1,0:T(8,128)(2,1)S(1)}, bf16[1280,640]{1,0:T(8,128)(2,1)}, u32[]{:S(2)}) copy-start(bf16[1280,640]{1,0:T(8,128)(2,1)} %get-tuple-element.1148) | copy-start | bytes 4915204 | tf_op jit(solution)/shard_map/while
  59.7 2.9 %collective-permute-start.1 = (bf16[640,1,128]{0,2,1:T(8,128)(2,1)}, bf16[640,1,128]{0,2,1:T(8,128)(2,1)S(1)}, u32[]{:S(2)}, u32[]{:S(2)}) collective-permute-start(bf16[640,1,128]{0,2,1:T(8,128)(2,1)} %get-tuple-element.1072), channel_id=1, source_target_pairs={{0,8},{8,0},{16,24},{24,16},{1,9},{9,1},{17,25},{25,17},{2,10},{10... | collective-permute-start | bytes 491528 | tf_op jit(solution)/shard_map/while/body/eval_jaxpr/ppermute | solution.py:22
  62.5 5.4 %collective-permute-start.2 = (bf16[640,1,128]{0,2,1:T(8,128)(2,1)S(1)}, bf16[640,1,128]{0,2,1:T(8,128)(2,1)S(1)}, u32[]{:S(2)}, u32[]{:S(2)}) collective-permute-start(bf16[640,1,128]{0,2,1:T(8,128)(2,1)S(1)} %collective-permute-done.1), channel_id=1, source_target_pairs={{0,16},{16,0},{8,24},{24,8},{1,17},{17,1},{9,25},{25,9},{2,18},{18... | collective-permute-start | bytes 491528 | tf_op jit(solution)/shard_map/while/body/eval_jaxpr/ppermute | solution.py:22
  63.7 5.9 %collective-permute-start = (bf16[640,1,128]{0,2,1:T(8,128)(2,1)}, bf16[640,1,128]{0,2,1:T(8,128)(2,1)S(1)}, u32[]{:S(2)}, u32[]{:S(2)}) collective-permute-start(bf16[640,1,128]{0,2,1:T(8,128)(2,1)} %get-tuple-element.1072), channel_id=1, source_target_pairs={{0,8},{8,16},{16,24},{1,9},{9,17},{17,25},{2,10},{10,18},{18,26},{... | collective-permute-start | bytes 491528 | tf_op jit(solution)/shard_map/while/body/eval_jaxpr/ppermute | solution.py:12
  69.6 10.4 %copy-start.1 = (bf16[1280,640]{1,0:T(8,128)(2,1)S(1)}, bf16[1280,640]{1,0:T(8,128)(2,1)}, u32[]{:S(2)}) copy-start(bf16[1280,640]{1,0:T(8,128)(2,1)} %get-tuple-element.1148) | copy-start | bytes 4915204 | tf_op jit(solution)/shard_map/while
  81.1 1.7 %collective-permute-start.1 = (bf16[640,1,128]{0,2,1:T(8,128)(2,1)}, bf16[640,1,128]{0,2,1:T(8,128)(2,1)S(1)}, u32[]{:S(2)}, u32[]{:S(2)}) collective-permute-start(bf16[640,1,128]{0,2,1:T(8,128)(2,1)} %get-tuple-element.1072), channel_id=1, source_target_pairs={{0,8},{8,0},{16,24},{24,16},{1,9},{9,1},{17,25},{25,17},{2,10},{10... | collective-permute-start | bytes 491528 | tf_op jit(solution)/shard_map/while/body/eval_jaxpr/ppermute | solution.py:22
  82.9 5.4 %collective-permute-start.2 = (bf16[640,1,128]{0,2,1:T(8,128)(2,1)S(1)}, bf16[640,1,128]{0,2,1:T(8,128)(2,1)S(1)}, u32[]{:S(2)}, u32[]{:S(2)}) collective-permute-start(bf16[640,1,128]{0,2,1:T(8,128)(2,1)S(1)} %collective-permute-done.1), channel_id=1, source_target_pairs={{0,16},{16,0},{8,24},{24,8},{1,17},{17,1},{9,25},{25,9},{2,18},{18... | collective-permute-start | bytes 491528 | tf_op jit(solution)/shard_map/while/body/eval_jaxpr/ppermute | solution.py:22
  84.1 5.9 %collective-permute-start = (bf16[640,1,128]{0,2,1:T(8,128)(2,1)}, bf16[640,1,128]{0,2,1:T(8,128)(2,1)S(1)}, u32[]{:S(2)}, u32[]{:S(2)}) collective-permute-start(bf16[640,1,128]{0,2,1:T(8,128)(2,1)} %get-tuple-element.1072), channel_id=1, source_target_pairs={{0,8},{8,16},{16,24},{1,9},{9,17},{17,25},{2,10},{10,18},{18,26},{... | collective-permute-start | bytes 491528 | tf_op jit(solution)/shard_map/while/body/eval_jaxpr/ppermute | solution.py:12
  90.0 10.4 %copy-start.1 = (bf16[1280,640]{1,0:T(8,128)(2,1)S(1)}, bf16[1280,640]{1,0:T(8,128)(2,1)}, u32[]{:S(2)}) copy-start(bf16[1280,640]{1,0:T(8,128)(2,1)} %get-tuple-element.1148) | copy-start | bytes 4915204 | tf_op jit(solution)/shard_map/while
  101.5 1.7 %collective-permute-start.1 = (bf16[640,1,128]{0,2,1:T(8,128)(2,1)}, bf16[640,1,128]{0,2,1:T(8,128)(2,1)S(1)}, u32[]{:S(2)}, u32[]{:S(2)}) collective-permute-start(bf16[640,1,128]{0,2,1:T(8,128)(2,1)} %get-tuple-element.1072), channel_id=1, source_target_pairs={{0,8},{8,0},{16,24},{24,16},{1,9},{9,1},{17,25},{25,17},{2,10},{10... | collective-permute-start | bytes 491528 | tf_op jit(solution)/shard_map/while/body/eval_jaxpr/ppermute | solution.py:22
  103.2 5.4 %collective-permute-start.2 = (bf16[640,1,128]{0,2,1:T(8,128)(2,1)S(1)}, bf16[640,1,128]{0,2,1:T(8,128)(2,1)S(1)}, u32[]{:S(2)}, u32[]{:S(2)}) collective-permute-start(bf16[640,1,128]{0,2,1:T(8,128)(2,1)S(1)} %collective-permute-done.1), channel_id=1, source_target_pairs={{0,16},{16,0},{8,24},{24,8},{1,17},{17,1},{9,25},{25,9},{2,18},{18... | collective-permute-start | bytes 491528 | tf_op jit(solution)/shard_map/while/body/eval_jaxpr/ppermute | solution.py:22
  104.4 5.9 %collective-permute-start = (bf16[640,1,128]{0,2,1:T(8,128)(2,1)}, bf16[640,1,128]{0,2,1:T(8,128)(2,1)S(1)}, u32[]{:S(2)}, u32[]{:S(2)}) collective-permute-start(bf16[640,1,128]{0,2,1:T(8,128)(2,1)} %get-tuple-element.1072), channel_id=1, source_target_pairs={{0,8},{8,16},{16,24},{1,9},{9,17},{17,25},{2,10},{10,18},{18,26},{... | collective-permute-start | bytes 491528 | tf_op jit(solution)/shard_map/while/body/eval_jaxpr/ppermute | solution.py:12
  110.3 10.4 %copy-start.2 = (bf16[1280,640]{1,0:T(8,128)(2,1)S(1)}, bf16[1280,640]{1,0:T(8,128)(2,1)}, u32[]{:S(2)}) copy-start(bf16[1280,640]{1,0:T(8,128)(2,1)} %get-tuple-element.1207) | copy-start | bytes 4915204 | tf_op jit(solution)/shard_map/while
  121.8 6.0 %collective-permute-start.3 = (bf16[640,1,128]{0,2,1:T(8,128)(2,1)}, bf16[640,1,128]{0,2,1:T(8,128)(2,1)S(1)}, u32[]{:S(2)}, u32[]{:S(2)}) collective-permute-start(bf16[640,1,128]{0,2,1:T(8,128)(2,1)} %get-tuple-element.1093), channel_id=1, source_target_pairs={{0,8},{8,16},{16,24},{1,9},{9,17},{17,25},{2,10},{10,18},{18,26},{... | collective-permute-start | bytes 491528 | tf_op jit(solution)/shard_map/while/body/eval_jaxpr/ppermute | solution.py:12
  127.9 8.5 %copy-start.2 = (bf16[1280,640]{1,0:T(8,128)(2,1)S(1)}, bf16[1280,640]{1,0:T(8,128)(2,1)}, u32[]{:S(2)}) copy-start(bf16[1280,640]{1,0:T(8,128)(2,1)} %get-tuple-element.1207) | copy-start | bytes 4915204 | tf_op jit(solution)/shard_map/while
  137.5 8.0 %collective-permute-start.3 = (bf16[640,1,128]{0,2,1:T(8,128)(2,1)}, bf16[640,1,128]{0,2,1:T(8,128)(2,1)S(1)}, u32[]{:S(2)}, u32[]{:S(2)}) collective-permute-start(bf16[640,1,128]{0,2,1:T(8,128)(2,1)} %get-tuple-element.1093), channel_id=1, source_target_pairs={{0,8},{8,16},{16,24},{1,9},{9,17},{17,25},{2,10},{10,18},{18,26},{... | collective-permute-start | bytes 491528 | tf_op jit(solution)/shard_map/while/body/eval_jaxpr/ppermute | solution.py:12
Sparse Core Ops, SparseCore 0:
  8.9 40.1 all-gather.2
where the time goes:
time: 154 us; the launch traced here: 153 us
  waiting for transfers between devices  58.7 us (38%)
  blocking collectives  30.9 us (20%)
  starting transfers between devices  23.2 us (15%)
  between operations  14.1 us (9%)
  loops' own time  10 us (6%)
  matrix products  5.6 us (4%)
  other arithmetic  5.39 us (4%)
  local copies, waits for them, and re-layouts  5.24 us (3%)
    all_gather x1, waiting for transfers between devices, per_device(): matrix_cols = lax.all_gather(weights[0], 'row', axis=0, tiled=True)  40 us
    all_gather x5, blocking collectives, advance(): lax.all_gather(activate(current, tap_mine, embed_mine, dilation, frame_co...  30.9 us
    ppermute x5, starting transfers between devices, shifted(): lax.ppermute(value, axis, [(source, source + steps) for source in range(f...  17 us
    ppermute x5, waiting for transfers between devices, shifted(): lax.ppermute(value, axis, [(source, source + steps) for source in range(f...  9.91 us
    ppermute x6, waiting for transfers between devices, from_partner(): return lax.ppermute(block, axis, route)  8.13 us
    ppermute x6, starting transfers between devices, from_partner(): return lax.ppermute(block, axis, route)  6.22 us
    another operation x1, loops' own time, per_device(): lax.fori_loop(0, first_end, lambda tick_id, carried: advance(tick_id, car...  6.05 us
    dot_general x5, matrix products, advance(): lax.dot_general(matrix_cols, activated.reshape(activated.shape[0], -1), (...  5.6 us
  transfers between devices with their start and end apart: 12, of which 12 were waited for; matrix products, arithmetic and copies ran while one was open for 1% of the time, Pallas kernels for 0%

commit v1 on v0

--- a/solution.py
+++ b/solution.py
@@ -45,7 +45,15 @@
     frame_count = latents.shape[3]
     midpoint = section_count // 2
     bit_total = section_count.bit_length() - 1
-    matrix_cols = lax.all_gather(weights[0], "row", axis=0, tiled=True)
+    frame_in = weights[0]
+    k_all = lax.axis_size("row")
+    panels = tuple(((s, (s + 1) % k_all) for s in range(k_all)))
+    v_now = [None] * k_all
+    v_now[k_all - 1] = frame_in
+    for k0 in range(k_all - 2, -1, -1):
+        v_now[k0] = lax.ppermute(v_now[k0 + 1], axis_name="row", perm=panels)
+    left_arr = jnp.concatenate(v_now, axis=0)
+    matrix_cols = jnp.roll(left_arr, shift=(lax.axis_index("row") + 1) * frame_in.shape[0], axis=0)
     tap_all = taps[0]
     time_rows = time_table[0]
     dilation = dilations[0]

time: 154 us -> 136 us (0.88)
  between operations: 14.1 us -> 0.84 us
  waiting for transfers between devices: 58.7 us -> 49.3 us
  starting transfers between devices: 23.2 us -> 28.2 us
    all_gather x1 -> x0, waiting for transfers between devices: 40 us -> none  [per_device(): matrix_cols = lax.all_gather(weights[0], 'row', axis=0, tiled=True)]
    ppermute x0 -> x3, waiting for transfers between devices: none -> 31.7 us  [per_device(): v_now[k0] = lax.ppermute(v_now[k0 + 1], axis_name='row', perm=panels)]
    ppermute x6, starting transfers between devices: 6.22 us -> 8.71 us  [from_partner(): return lax.ppermute(block, axis, route)]
    ppermute x0 -> x3, starting transfers between devices: none -> 2.13 us  [per_device(): v_now[k0] = lax.ppermute(v_now[k0 + 1], axis_name='row', perm=panels)]
  transfers between devices with their start and end apart: 12 -> 14, of which waited for: 12 -> 14; matrix products, arithmetic and copies ran while one was open for 1% -> 1% of each run, Pallas kernels for 0% -> 0%
where the time goes in v1:
time: 136 us; the launch traced here: 135 us
  waiting for transfers between devices  49.3 us (36%)
  blocking collectives  29.7 us (22%)
  starting transfers between devices  28.2 us (21%)
  loops' own time  9.98 us (7%)
  local copies, waits for them, and re-layouts  6.04 us (4%)
  matrix products  5.62 us (4%)
  other arithmetic  5.39 us (4%)
    ppermute x3, waiting for transfers between devices, per_device(): v_now[k0] = lax.ppermute(v_now[k0 + 1], axis_name='row', perm=panels)  31.7 us
    all_gather x5, blocking collectives, advance(): lax.all_gather(activate(current, tap_mine, embed_mine, dilation, frame_co...  29.7 us
    ppermute x5, starting transfers between devices, shifted(): lax.ppermute(value, axis, [(source, source + steps) for source in range(f...  17.4 us
    ppermute x5, waiting for transfers between devices, shifted(): lax.ppermute(value, axis, [(source, source + steps) for source in range(f...  9.5 us
    ppermute x6, starting transfers between devices, from_partner(): return lax.ppermute(block, axis, route)  8.71 us
    ppermute x6, waiting for transfers between devices, from_partner(): return lax.ppermute(block, axis, route)  8.13 us
    another operation x1, loops' own time, per_device(): lax.fori_loop(0, first_end, lambda tick_id, carried: advance(tick_id, car...  6.02 us
    dot_general x5, matrix products, advance(): lax.dot_general(matrix_cols, activated.reshape(activated.shape[0], -1), (...  5.62 us
  transfers between devices with their start and end apart: 14, of which 14 were waited for; matrix products, arithmetic and copies ran while one was open for 1% of the time, Pallas kernels for 0%

profile of v1, /device:TPU:1, one launch (start us, length us, event | category | flops | bytes accessed | tf_op | source)
XLA Modules:
  0.0 135.1 jit_solution(2101420674557445147)
XLA Ops:
  0.0 2.1 %collective-permute-start.4 = (bf16[320,640]{1,0:T(8,128)(2,1)}, bf16[320,640]{1,0:T(8,128)(2,1)S(1)}, u32[]{:S(2)}, u32[]{:S(2)}) collective-permute-start(bf16[320,640]{1,0:T(8,128)(2,1)} %bitcast.104), channel_id=1, source_target_pairs={{0,2},{2,4},{4,6},{6,0},{1,3},{3,5},{5,7},{7,1},{8,10},{10,12},{12... | collective-permute-start | bytes 1228808 | tf_op jit(solution)/shard_map/ppermute | solution.py:54
  2.1 11.5 %collective-permute-done.4 = bf16[320,640]{1,0:T(8,128)(2,1)S(1)} collective-permute-done((bf16[320,640]{1,0:T(8,128)(2,1)}, bf16[320,640]{1,0:T(8,128)(2,1)S(1)}, u32[]{:S(2)}, u32[]{:S(2)}) %collective-permute-start.4) | collective-permute-done | bytes 409632 | tf_op jit(solution)/shard_map/ppermute | solution.py:54
  13.6 11.5 %collective-permute-done.5 = bf16[320,640]{1,0:T(8,128)(2,1)S(1)} collective-permute-done((bf16[320,640]{1,0:T(8,128)(2,1)S(1)}, bf16[320,640]{1,0:T(8,128)(2,1)S(1)}, u32[]{:S(2)}, u32[]{:S(2)}) %collective-permute-start.5) | collective-permute-done | bytes 409632 | tf_op jit(solution)/shard_map/ppermute | solution.py:54
  25.8 1.2 copy.7
  27.0 8.7 %collective-permute-done.6 = bf16[320,640]{1,0:T(8,128)(2,1)S(1)} collective-permute-done((bf16[320,640]{1,0:T(8,128)(2,1)S(1)}, bf16[320,640]{1,0:T(8,128)(2,1)S(1)}, u32[]{:S(2)}, u32[]{:S(2)}) %collective-permute-start.6) | collective-permute-done | bytes 409632 | tf_op jit(solution)/shard_map/ppermute | solution.py:54
  36.7 62.4 %while.38 = (s32[]{:T(128)}, bf16[640,1,128]{0,2,1:T(8,128)(2,1)S(1)}, bf16[2,640,1,128]{1,3,2,0:T(8,128)(2,1)S(1)}, bf16[2,640,1,128]{1,3,2,0:T(8,128)(2,1)S(1)...) while((s32[]{:T(128)}, ...), condition=%wide.region_1.2_spmd, body=%wide.region_0.1_spmd.sunk | while | flops 211354256 | bytes 7730424 | solution.py:119
  36.7 0.6 dynamic_slice.280
  39.3 0.8 slice_reduce_fusion.8
  40.3 4.8 %all_gather.24 = bf16[1280,1,128]{0,2,1:T(8,128)(2,1)S(1)} all-gather(bf16[640,1,128]{0,2,1:T(8,128)(2,1)S(1)} %multiply_convert_fusion.4), channel_id=1, replica_groups=mesh['section'=4,'row'=4,'col'=2] {'col'}, dimensions={0}, use_global_device_ids=true | all-gather | bytes 491520 | tf_op jit(solution)/shard_map/while/body/eval_jaxpr/all_gather | solution.py:76
  45.2 1.1 bitcast_dynamic-update-slice_fusion.6
  46.3 4.2 %collective-permute-start.1 = (bf16[640,1,128]{0,2,1:T(8,128)(2,1)}, bf16[640,1,128]{0,2,1:T(8,128)(2,1)S(1)}, u32[]{:S(2)}, u32[]{:S(2)}) collective-permute-start(bf16[640,1,128]{0,2,1:T(8,128)(2,1)} %get-tuple-element.1072), channel_id=1, source_target_pairs={{0,8},{8,0},{16,24},{24,16},{1,9},{9,1},{17,25},{25,17},{2,10},{10... | collective-permute-start | bytes 491528 | tf_op jit(solution)/shard_map/while/body/eval_jaxpr/ppermute | solution.py:22
  50.5 1.2 collective-permute-done.1
  51.8 0.8 collective-permute-start.2
  52.6 3.1 %collective-permute-start = (bf16[640,1,128]{0,2,1:T(8,128)(2,1)}, bf16[640,1,128]{0,2,1:T(8,128)(2,1)S(1)}, u32[]{:S(2)}, u32[]{:S(2)}) collective-permute-start(bf16[640,1,128]{0,2,1:T(8,128)(2,1)} %get-tuple-element.1072), channel_id=1, source_target_pairs={{0,8},{8,16},{16,24},{1,9},{9,17},{17,25},{2,10},{10,18},{18,26},{... | collective-permute-start | bytes 491528 | tf_op jit(solution)/shard_map/while/body/eval_jaxpr/ppermute | solution.py:12
  55.7 1.5 %collective-permute-done.2 = bf16[640,1,128]{0,2,1:T(8,128)(2,1)S(1)} collective-permute-done((bf16[640,1,128]{0,2,1:T(8,128)(2,1)S(1)}, bf16[640,1,128]{0,2,1:T(8,128)(2,1)S(1)}, u32[]{:S(2)}, u32[]{:S(2)}) %collective-permute-start.2) | collective-permute-done | bytes 163872 | tf_op jit(solution)/shard_map/while/body/eval_jaxpr/ppermute | solution.py:22
  57.3 1.2 collective-permute-done
  58.5 0.6 dynamic_slice.280
  61.0 0.8 slice_reduce_fusion.8
  62.0 6.5 %all_gather.24 = bf16[1280,1,128]{0,2,1:T(8,128)(2,1)S(1)} all-gather(bf16[640,1,128]{0,2,1:T(8,128)(2,1)S(1)} %multiply_convert_fusion.4), channel_id=1, replica_groups=mesh['section'=4,'row'=4,'col'=2] {'col'}, dimensions={0}, use_global_device_ids=true | all-gather | bytes 491520 | tf_op jit(solution)/shard_map/while/body/eval_jaxpr/all_gather | solution.py:76
  68.5 1.1 bitcast_dynamic-update-slice_fusion.6
  69.6 0.8 collective-permute-start.1
  70.5 1.2 collective-permute-done.1
  71.7 1.2 collective-permute-start.2
  72.9 2.7 %collective-permute-start = (bf16[640,1,128]{0,2,1:T(8,128)(2,1)}, bf16[640,1,128]{0,2,1:T(8,128)(2,1)S(1)}, u32[]{:S(2)}, u32[]{:S(2)}) collective-permute-start(bf16[640,1,128]{0,2,1:T(8,128)(2,1)} %get-tuple-element.1072), channel_id=1, source_target_pairs={{0,8},{8,16},{16,24},{1,9},{9,17},{17,25},{2,10},{10,18},{18,26},{... | collective-permute-start | bytes 491528 | tf_op jit(solution)/shard_map/while/body/eval_jaxpr/ppermute | solution.py:12
  75.7 1.5 %collective-permute-done.2 = bf16[640,1,128]{0,2,1:T(8,128)(2,1)S(1)} collective-permute-done((bf16[640,1,128]{0,2,1:T(8,128)(2,1)S(1)}, bf16[640,1,128]{0,2,1:T(8,128)(2,1)S(1)}, u32[]{:S(2)}, u32[]{:S(2)}) %collective-permute-start.2) | collective-permute-done | bytes 163872 | tf_op jit(solution)/shard_map/while/body/eval_jaxpr/ppermute | solution.py:22
  77.2 1.6 %collective-permute-done = bf16[640,1,128]{0,2,1:T(8,128)(2,1)S(1)} collective-permute-done((bf16[640,1,128]{0,2,1:T(8,128)(2,1)}, bf16[640,1,128]{0,2,1:T(8,128)(2,1)S(1)}, u32[]{:S(2)}, u32[]{:S(2)}) %collective-permute-start) | collective-permute-done | bytes 163872 | tf_op jit(solution)/shard_map/while/body/eval_jaxpr/ppermute | solution.py:12
  78.8 0.6 dynamic_slice.280
  81.3 0.8 slice_reduce_fusion.8
  82.4 6.8 %all_gather.24 = bf16[1280,1,128]{0,2,1:T(8,128)(2,1)S(1)} all-gather(bf16[640,1,128]{0,2,1:T(8,128)(2,1)S(1)} %multiply_convert_fusion.4), channel_id=1, replica_groups=mesh['section'=4,'row'=4,'col'=2] {'col'}, dimensions={0}, use_global_device_ids=true | all-gather | bytes 491520 | tf_op jit(solution)/shard_map/while/body/eval_jaxpr/all_gather | solution.py:76
  89.2 1.1 bitcast_dynamic-update-slice_fusion.6
  90.8 1.2 collective-permute-done.1
  92.0 1.2 collective-permute-start.2
  93.2 2.7 %collective-permute-start = (bf16[640,1,128]{0,2,1:T(8,128)(2,1)}, bf16[640,1,128]{0,2,1:T(8,128)(2,1)S(1)}, u32[]{:S(2)}, u32[]{:S(2)}) collective-permute-start(bf16[640,1,128]{0,2,1:T(8,128)(2,1)} %get-tuple-element.1072), channel_id=1, source_target_pairs={{0,8},{8,16},{16,24},{1,9},{9,17},{17,25},{2,10},{10,18},{18,26},{... | collective-permute-start | bytes 491528 | tf_op jit(solution)/shard_map/while/body/eval_jaxpr/ppermute | solution.py:12
  96.0 1.5 %collective-permute-done.2 = bf16[640,1,128]{0,2,1:T(8,128)(2,1)S(1)} collective-permute-done((bf16[640,1,128]{0,2,1:T(8,128)(2,1)S(1)}, bf16[640,1,128]{0,2,1:T(8,128)(2,1)S(1)}, u32[]{:S(2)}, u32[]{:S(2)}) %collective-permute-start.2) | collective-permute-done | bytes 163872 | tf_op jit(solution)/shard_map/while/body/eval_jaxpr/ppermute | solution.py:22
  97.5 1.6 %collective-permute-done = bf16[640,1,128]{0,2,1:T(8,128)(2,1)S(1)} collective-permute-done((bf16[640,1,128]{0,2,1:T(8,128)(2,1)}, bf16[640,1,128]{0,2,1:T(8,128)(2,1)S(1)}, u32[]{:S(2)}, u32[]{:S(2)}) %collective-permute-start) | collective-permute-done | bytes 163872 | tf_op jit(solution)/shard_map/while/body/eval_jaxpr/ppermute | solution.py:12
  99.1 35.1 %while.39 = (s32[]{:T(128)}, bf16[640,1,128]{0,2,1:T(8,128)(2,1)S(1)}, bf16[2,640,1,128]{1,3,2,0:T(8,128)(2,1)S(1)}, pred[]{:T(512)}, s32[]{:T(128)}, /*index=5*...) while((s32[]{:T(128)}, ...), condition=%wide.region_3.4_spmd, body=%wide.region_2.3_spmd.sunk | while | flops 211272336 | bytes 5600367 | solution.py:122
  99.1 0.6 dynamic_slice.285
  101.7 0.8 slice_reduce_fusion.9
  102.7 6.8 %all_gather.25 = bf16[1280,1,128]{0,2,1:T(8,128)(2,1)S(1)} all-gather(bf16[640,1,128]{0,2,1:T(8,128)(2,1)S(1)} %multiply_convert_fusion.5), channel_id=1, replica_groups=mesh['section'=4,'row'=4,'col'=2] {'col'}, dimensions={0}, use_global_device_ids=true | all-gather | bytes 491520 | tf_op jit(solution)/shard_map/while/body/eval_jaxpr/all_gather | solution.py:76
  109.5 1.1 bitcast_dynamic-update-slice_fusion.8
  110.6 3.5 %collective-permute-start.3 = (bf16[640,1,128]{0,2,1:T(8,128)(2,1)}, bf16[640,1,128]{0,2,1:T(8,128)(2,1)S(1)}, u32[]{:S(2)}, u32[]{:S(2)}) collective-permute-start(bf16[640,1,128]{0,2,1:T(8,128)(2,1)} %get-tuple-element.1093), channel_id=1, source_target_pairs={{0,8},{8,16},{16,24},{1,9},{9,17},{17,25},{2,10},{10,18},{18,26},{... | collective-permute-start | bytes 491528 | tf_op jit(solution)/shard_map/while/body/eval_jaxpr/ppermute | solution.py:12
  114.1 2.6 %collective-permute-done.3 = bf16[640,1,128]{0,2,1:T(8,128)(2,1)S(1)} collective-permute-done((bf16[640,1,128]{0,2,1:T(8,128)(2,1)}, bf16[640,1,128]{0,2,1:T(8,128)(2,1)S(1)}, u32[]{:S(2)}, u32[]{:S(2)}) %collective-permute-start.3) | collective-permute-done | bytes 163872 | tf_op jit(solution)/shard_map/while/body/eval_jaxpr/ppermute | solution.py:12
  119.2 0.8 slice_reduce_fusion.9
  120.2 4.8 %all_gather.25 = bf16[1280,1,128]{0,2,1:T(8,128)(2,1)S(1)} all-gather(bf16[640,1,128]{0,2,1:T(8,128)(2,1)S(1)} %multiply_convert_fusion.5), channel_id=1, replica_groups=mesh['section'=4,'row'=4,'col'=2] {'col'}, dimensions={0}, use_global_device_ids=true | all-gather | bytes 491520 | tf_op jit(solution)/shard_map/while/body/eval_jaxpr/all_gather | solution.py:76
  125.1 1.1 bitcast_dynamic-update-slice_fusion.8
  126.2 5.4 %collective-permute-start.3 = (bf16[640,1,128]{0,2,1:T(8,128)(2,1)}, bf16[640,1,128]{0,2,1:T(8,128)(2,1)S(1)}, u32[]{:S(2)}, u32[]{:S(2)}) collective-permute-start(bf16[640,1,128]{0,2,1:T(8,128)(2,1)} %get-tuple-element.1093), channel_id=1, source_target_pairs={{0,8},{8,16},{16,24},{1,9},{9,17},{17,25},{2,10},{10,18},{18,26},{... | collective-permute-start | bytes 491528 | tf_op jit(solution)/shard_map/while/body/eval_jaxpr/ppermute | solution.py:12
  131.7 2.6 %collective-permute-done.3 = bf16[640,1,128]{0,2,1:T(8,128)(2,1)S(1)} collective-permute-done((bf16[640,1,128]{0,2,1:T(8,128)(2,1)}, bf16[640,1,128]{0,2,1:T(8,128)(2,1)S(1)}, u32[]{:S(2)}, u32[]{:S(2)}) %collective-permute-start.3) | collective-permute-done | bytes 163872 | tf_op jit(solution)/shard_map/while/body/eval_jaxpr/ppermute | solution.py:12
  134.2 0.9 copy.9
  (45 shorter events, 3.4 us)
Async XLA Ops:
  0.0 25.8 %copy-start = (f32[1,3,1280]{2,0,1:T(1,128)S(1)}, f32[1,3,1280]{2,0,1:T(1,128)}, u32[]{:S(2)}) copy-start(f32[1,3,1280]{2,0,1:T(1,128)} %param.13) | copy-start | bytes 46084
  0.0 35.9 %copy-start.1 = (bf16[1,320,640]{2,1,0:T(8,128)(2,1)S(1)}, bf16[1,320,640]{2,1,0:T(8,128)(2,1)}, u32[]{:S(2)}) copy-start(bf16[1,320,640]{2,1,0:T(8,128)(2,1)} %param.12) | copy-start | bytes 1228804
  0.0 13.6 %collective-permute-start.4 = (bf16[320,640]{1,0:T(8,128)(2,1)}, bf16[320,640]{1,0:T(8,128)(2,1)S(1)}, u32[]{:S(2)}, u32[]{:S(2)}) collective-permute-start(bf16[320,640]{1,0:T(8,128)(2,1)} %bitcast.104), channel_id=1, source_target_pairs={{0,2},{2,4},{4,6},{6,0},{1,3},{3,5},{5,7},{7,1},{8,10},{10,12},{12... | collective-permute-start | bytes 1228808 | tf_op jit(solution)/shard_map/ppermute | solution.py:54
  13.6 11.5 %collective-permute-start.5 = (bf16[320,640]{1,0:T(8,128)(2,1)S(1)}, bf16[320,640]{1,0:T(8,128)(2,1)S(1)}, u32[]{:S(2)}, u32[]{:S(2)}) collective-permute-start(bf16[320,640]{1,0:T(8,128)(2,1)S(1)} %collective-permute-done.4), channel_id=1, source_target_pairs={{0,2},{2,4},{4,6},{6,0},{1,3},{3,5},{5,7},{7,1},{8,10},{10,12},{12... | collective-permute-start | bytes 1228808 | tf_op jit(solution)/shard_map/ppermute | solution.py:54
  25.1 10.6 %collective-permute-start.6 = (bf16[320,640]{1,0:T(8,128)(2,1)S(1)}, bf16[320,640]{1,0:T(8,128)(2,1)S(1)}, u32[]{:S(2)}, u32[]{:S(2)}) collective-permute-start(bf16[320,640]{1,0:T(8,128)(2,1)S(1)} %collective-permute-done.5), channel_id=1, source_target_pairs={{0,2},{2,4},{4,6},{6,0},{1,3},{3,5},{5,7},{7,1},{8,10},{10,12},{12... | collective-permute-start | bytes 1228808 | tf_op jit(solution)/shard_map/ppermute | solution.py:54
  36.0 0.7 copy-start.2
  46.3 5.5 %collective-permute-start.1 = (bf16[640,1,128]{0,2,1:T(8,128)(2,1)}, bf16[640,1,128]{0,2,1:T(8,128)(2,1)S(1)}, u32[]{:S(2)}, u32[]{:S(2)}) collective-permute-start(bf16[640,1,128]{0,2,1:T(8,128)(2,1)} %get-tuple-element.1072), channel_id=1, source_target_pairs={{0,8},{8,0},{16,24},{24,16},{1,9},{9,1},{17,25},{25,17},{2,10},{10... | collective-permute-start | bytes 491528 | tf_op jit(solution)/shard_map/while/body/eval_jaxpr/ppermute | solution.py:22
  51.8 5.4 %collective-permute-start.2 = (bf16[640,1,128]{0,2,1:T(8,128)(2,1)S(1)}, bf16[640,1,128]{0,2,1:T(8,128)(2,1)S(1)}, u32[]{:S(2)}, u32[]{:S(2)}) collective-permute-start(bf16[640,1,128]{0,2,1:T(8,128)(2,1)S(1)} %collective-permute-done.1), channel_id=1, source_target_pairs={{0,16},{16,0},{8,24},{24,8},{1,17},{17,1},{9,25},{25,9},{2,18},{18... | collective-permute-start | bytes 491528 | tf_op jit(solution)/shard_map/while/body/eval_jaxpr/ppermute | solution.py:22
  52.6 5.9 %collective-permute-start = (bf16[640,1,128]{0,2,1:T(8,128)(2,1)}, bf16[640,1,128]{0,2,1:T(8,128)(2,1)S(1)}, u32[]{:S(2)}, u32[]{:S(2)}) collective-permute-start(bf16[640,1,128]{0,2,1:T(8,128)(2,1)} %get-tuple-element.1072), channel_id=1, source_target_pairs={{0,8},{8,16},{16,24},{1,9},{9,17},{17,25},{2,10},{10,18},{18,26},{... | collective-permute-start | bytes 491528 | tf_op jit(solution)/shard_map/while/body/eval_jaxpr/ppermute | solution.py:12
  69.6 2.1 %collective-permute-start.1 = (bf16[640,1,128]{0,2,1:T(8,128)(2,1)}, bf16[640,1,128]{0,2,1:T(8,128)(2,1)S(1)}, u32[]{:S(2)}, u32[]{:S(2)}) collective-permute-start(bf16[640,1,128]{0,2,1:T(8,128)(2,1)} %get-tuple-element.1072), channel_id=1, source_target_pairs={{0,8},{8,0},{16,24},{24,16},{1,9},{9,1},{17,25},{25,17},{2,10},{10... | collective-permute-start | bytes 491528 | tf_op jit(solution)/shard_map/while/body/eval_jaxpr/ppermute | solution.py:22
  71.7 5.4 %collective-permute-start.2 = (bf16[640,1,128]{0,2,1:T(8,128)(2,1)S(1)}, bf16[640,1,128]{0,2,1:T(8,128)(2,1)S(1)}, u32[]{:S(2)}, u32[]{:S(2)}) collective-permute-start(bf16[640,1,128]{0,2,1:T(8,128)(2,1)S(1)} %collective-permute-done.1), channel_id=1, source_target_pairs={{0,16},{16,0},{8,24},{24,8},{1,17},{17,1},{9,25},{25,9},{2,18},{18... | collective-permute-start | bytes 491528 | tf_op jit(solution)/shard_map/while/body/eval_jaxpr/ppermute | solution.py:22
  72.9 5.9 %collective-permute-start = (bf16[640,1,128]{0,2,1:T(8,128)(2,1)}, bf16[640,1,128]{0,2,1:T(8,128)(2,1)S(1)}, u32[]{:S(2)}, u32[]{:S(2)}) collective-permute-start(bf16[640,1,128]{0,2,1:T(8,128)(2,1)} %get-tuple-element.1072), channel_id=1, source_target_pairs={{0,8},{8,16},{16,24},{1,9},{9,17},{17,25},{2,10},{10,18},{18,26},{... | collective-permute-start | bytes 491528 | tf_op jit(solution)/shard_map/while/body/eval_jaxpr/ppermute | solution.py:12
  90.3 1.7 %collective-permute-start.1 = (bf16[640,1,128]{0,2,1:T(8,128)(2,1)}, bf16[640,1,128]{0,2,1:T(8,128)(2,1)S(1)}, u32[]{:S(2)}, u32[]{:S(2)}) collective-permute-start(bf16[640,1,128]{0,2,1:T(8,128)(2,1)} %get-tuple-element.1072), channel_id=1, source_target_pairs={{0,8},{8,0},{16,24},{24,16},{1,9},{9,1},{17,25},{25,17},{2,10},{10... | collective-permute-start | bytes 491528 | tf_op jit(solution)/shard_map/while/body/eval_jaxpr/ppermute | solution.py:22
  92.0 5.4 %collective-permute-start.2 = (bf16[640,1,128]{0,2,1:T(8,128)(2,1)S(1)}, bf16[640,1,128]{0,2,1:T(8,128)(2,1)S(1)}, u32[]{:S(2)}, u32[]{:S(2)}) collective-permute-start(bf16[640,1,128]{0,2,1:T(8,128)(2,1)S(1)} %collective-permute-done.1), channel_id=1, source_target_pairs={{0,16},{16,0},{8,24},{24,8},{1,17},{17,1},{9,25},{25,9},{2,18},{18... | collective-permute-start | bytes 491528 | tf_op jit(solution)/shard_map/while/body/eval_jaxpr/ppermute | solution.py:22
  93.2 5.9 %collective-permute-start = (bf16[640,1,128]{0,2,1:T(8,128)(2,1)}, bf16[640,1,128]{0,2,1:T(8,128)(2,1)S(1)}, u32[]{:S(2)}, u32[]{:S(2)}) collective-permute-start(bf16[640,1,128]{0,2,1:T(8,128)(2,1)} %get-tuple-element.1072), channel_id=1, source_target_pairs={{0,8},{8,16},{16,24},{1,9},{9,17},{17,25},{2,10},{10,18},{18,26},{... | collective-permute-start | bytes 491528 | tf_op jit(solution)/shard_map/while/body/eval_jaxpr/ppermute | solution.py:12
  110.6 6.0 %collective-permute-start.3 = (bf16[640,1,128]{0,2,1:T(8,128)(2,1)}, bf16[640,1,128]{0,2,1:T(8,128)(2,1)S(1)}, u32[]{:S(2)}, u32[]{:S(2)}) collective-permute-start(bf16[640,1,128]{0,2,1:T(8,128)(2,1)} %get-tuple-element.1093), channel_id=1, source_target_pairs={{0,8},{8,16},{16,24},{1,9},{9,17},{17,25},{2,10},{10,18},{18,26},{... | collective-permute-start | bytes 491528 | tf_op jit(solution)/shard_map/while/body/eval_jaxpr/ppermute | solution.py:12
  126.2 8.0 %collective-permute-start.3 = (bf16[640,1,128]{0,2,1:T(8,128)(2,1)}, bf16[640,1,128]{0,2,1:T(8,128)(2,1)S(1)}, u32[]{:S(2)}, u32[]{:S(2)}) collective-permute-start(bf16[640,1,128]{0,2,1:T(8,128)(2,1)} %get-tuple-element.1093), channel_id=1, source_target_pairs={{0,8},{8,16},{16,24},{1,9},{9,17},{17,25},{2,10},{10,18},{18,26},{... | collective-permute-start | bytes 491528 | tf_op jit(solution)/shard_map/while/body/eval_jaxpr/ppermute | solution.py:12
